TPU v7x, 128 devices: a whole 4x4x4 slice. The times are simulated.
128 devices in a mesh: ctx: 64 (over y, z, x), head: 2 (over core).
Axes of the slice: x: 4, y: 4, z: 4, core: 2. Of those that a mesh axis runs over, the one named last changes fastest.
Arguments:
- queries: float32 [32768, 1024], P('ctx', 'head'), may hold values from -5 to 5
- keys: float32 [32768, 1024], P('ctx', 'head'), may hold values from -5 to 5
- values: float32 [32768, 1024], P('ctx', 'head'), may hold values from -6 to 6
- transitions: float32 [32768, 1024], P('ctx', 'head'), may hold values from -6 to 6
- betas: float32 [8, 32768], P('head', 'ctx'), may hold values from 0 to 2
- documents: int32 [32768], P('ctx'), may hold values from 0 to 31, never falling along the last dimension, each value on 1 to 2048 neighbouring positions
- out_weight: float32 [1024, 2048], P('head'), may hold values from -1.5 to 1.5
Outputs:
- output: float32 [32768, 2048], P(('ctx', 'head'))
Inputs may be any that keep to these rules, and one draw needn't show every extreme that they name: `documents`: document ids never fall along the tokens; every document holds at most 2048 tokens.
All inputs are finite; a program needn't handle non-finite values.
Results may differ from a plain program's by a relative error of at most 0.0003.
Values sent between devices are 32-bit elements; how exact they have to be, the bound alone decides.
A program may use at most 320 MiB of HBM per device.

v0:
```python
import math

import jax
import jax.numpy as jnp
from jax import lax
from jax.sharding import PartitionSpec as P

BLOCK_TOKENS = 512


HIGHEST = lax.Precision.HIGHEST


def passed_along(value, axis, steps):
    count = lax.axis_size(axis)
    leading, last = (max(0, -steps), min(count, count - steps))
    return lax.ppermute(value, axis, [(source, source + steps) for source in range(leading, last)])


def contract(pattern, left_operand, right_operand):
    return jnp.einsum(pattern, left_operand, right_operand, precision=HIGHEST)


def piece_length():
    return 128


def unit_lower_inverse(lower_mat):
    lead = lower_mat.shape[:-2]
    order = lower_mat.shape[-1]
    depth = len(lead)
    inverse_blocks = jnp.ones(lead + (order, 1, 1), jnp.float32)
    size = 1
    while size < order:
        count = order // (2 * size)
        tiled = lower_mat.reshape(lead + (count, 2, size, count, 2, size))
        diagonal_tiles = jnp.diagonal(tiled, axis1=depth, axis2=depth + 3)
        lower_left = jnp.moveaxis(diagonal_tiles[..., 1, :, 0, :, :], -1, depth)
        paired = inverse_blocks.reshape(lead + (count, 2, size, size))
        upper_inverse = paired[..., 0, :, :]
        lower_inverse = paired[..., 1, :, :]
        off_block = -contract(
            "...ij,...jk->...ik",
            lower_inverse,
            contract("...ij,...jk->...ik", lower_left, upper_inverse),
        )
        top_half = jnp.concatenate([upper_inverse, jnp.zeros_like(upper_inverse)], axis=-1)
        bottom_half = jnp.concatenate([off_block, lower_inverse], axis=-1)
        inverse_blocks = jnp.concatenate([top_half, bottom_half], axis=-2)
        size = size * 2
    return inverse_blocks.reshape(lead + (order, order))


def local_parts(queries, keys, transitions, betas):
    batches, length, groups, head_size = queries.shape
    piece_size = piece_length()
    pieces = length // piece_size
    sub_shape = (batches, pieces, piece_size, groups, head_size)
    unit_dirs = transitions * lax.rsqrt(
        jnp.sum(transitions * transitions, axis=-1, keepdims=True) + 1e-06
    )
    query_sub = queries.reshape(sub_shape)
    key_sub = keys.reshape(sub_shape)
    trans_sub = unit_dirs.reshape(sub_shape)
    beta_sub = jnp.transpose(betas.reshape(batches, pieces, piece_size, groups), (0, 1, 3, 2))
    row_ids = lax.broadcasted_iota(jnp.int32, (piece_size, piece_size), 0)
    col_ids = lax.broadcasted_iota(jnp.int32, (piece_size, piece_size), 1)
    strictly = row_ids > col_ids
    within = row_ids >= col_ids
    gram_matrix = contract("bnihd,bnjhd->bnhij", trans_sub, trans_sub)
    lower_mat = jnp.eye(piece_size, dtype=jnp.float32) + jnp.where(
        strictly, beta_sub[..., :, None] * gram_matrix, 0.0
    )
    beta_keys = jnp.where(
        strictly, beta_sub[..., :, None] * contract("bnihd,bnjhd->bnhij", trans_sub, key_sub), 0.0
    )
    beta_rows = beta_sub[..., None] * jnp.transpose(trans_sub, (0, 1, 3, 2, 4))
    inverse = unit_lower_inverse(lower_mat)
    solved = contract(
        "bnhij,bnhjk->bnhik", inverse, jnp.concatenate([beta_keys, beta_rows], axis=-1)
    )
    carried = solved[..., :piece_size]
    applied = solved[..., piece_size:]
    query_dirs = jnp.where(within, contract("bnihd,bnshd->bnhis", query_sub, trans_sub), 0.0)
    own_scores = contract("bnihd,bnjhd->bnhij", query_sub, key_sub) - contract(
        "bnhis,bnhsj->bnhij", query_dirs, carried
    )
    query_hat = jnp.transpose(query_sub, (0, 1, 3, 2, 4)) - contract(
        "bnhis,bnhsd->bnhid", query_dirs, applied
    )
    key_hat = jnp.transpose(key_sub, (0, 1, 3, 2, 4)) - contract(
        "bnhsj,bnshd->bnhjd", carried, trans_sub
    )
    sub_steps = jnp.eye(head_size, dtype=jnp.float32) - contract(
        "bnshe,bnhsf->bnhef", trans_sub, applied
    )
    return (query_hat, key_hat, own_scores, sub_steps)


def block_form(query_hat, key_hat, own_scores, sub_steps):
    batches, pieces, groups, piece_size, head_size = query_hat.shape
    rows_out = []
    queries_out = []
    for query_index in range(pieces):
        current = query_hat[:, query_index]
        tile_list = [own_scores[:, query_index]]
        for key_index in range(query_index - 1, -1, -1):
            tile_list.insert(0, contract("bhid,bhjd->bhij", current, key_hat[:, key_index]))
            current = contract("bhie,bhef->bhif", current, sub_steps[:, key_index])
        if query_index < pieces - 1:
            tile_list.append(
                jnp.zeros(
                    (batches, groups, piece_size, (pieces - 1 - query_index) * piece_size),
                    jnp.float32,
                )
            )
        rows_out.append(jnp.concatenate(tile_list, axis=-1))
        queries_out.append(current)
    intra_scores = jnp.concatenate(rows_out, axis=2)
    block_queries = jnp.stack(queries_out, axis=2).reshape(
        batches, groups, pieces * piece_size, head_size
    )
    suffix = jnp.broadcast_to(
        jnp.eye(head_size, dtype=jnp.float32), (batches, groups, head_size, head_size)
    )
    keys_out = [None] * pieces
    for key_index in range(pieces - 1, -1, -1):
        keys_out[key_index] = contract("bhef,bhjf->bhje", suffix, key_hat[:, key_index])
        suffix = contract("bhef,bhfg->bheg", suffix, sub_steps[:, key_index])
    block_keys = jnp.stack(keys_out, axis=2).reshape(
        batches, groups, pieces * piece_size, head_size
    )
    return (block_queries, block_keys, intra_scores, suffix)


def absorb(softmax_state, raw_scores, allowed, value_part):
    row_peak, row_total, summed = softmax_state
    masked = jnp.where(allowed, raw_scores, -jnp.inf)
    new_peak = jnp.maximum(row_peak, jnp.max(masked, axis=-1, keepdims=True))
    factor = jnp.exp(row_peak - new_peak)
    weights = jnp.where(allowed, jnp.exp(masked - new_peak), 0.0)
    row_total = row_total * factor + jnp.sum(weights, axis=-1, keepdims=True)
    summed = summed * factor + contract("...ij,...jd->...id", weights, value_part)
    return (new_peak, row_total, summed)


def shards(queries, keys, values, transitions, betas, documents, out_weight):
    groups = betas.shape[0]
    token_rows = queries.shape[0]
    head_size = queries.shape[1] // groups
    length = BLOCK_TOKENS
    blocks = token_rows // length
    block_shape = (blocks, length, groups, head_size)
    beta_blocks = jnp.transpose(betas.reshape(groups, blocks, length), (1, 2, 0))
    parts = local_parts(
        queries.reshape(block_shape),
        keys.reshape(block_shape),
        transitions.reshape(block_shape),
        beta_blocks,
    )
    block_queries, block_keys, intra_scores, block_steps = block_form(*parts)
    value_blocks = jnp.transpose(values.reshape(block_shape), (0, 2, 1, 3))
    document_blocks = documents.reshape(blocks, length)
    doc_float = document_blocks.astype(jnp.float32)
    identity = jnp.eye(head_size, dtype=jnp.float32)
    hop_total = (blocks + 2) // blocks
    received = []
    for hop_index in range(1, hop_total + 1):
        key_count = min(blocks, 3 - (hop_index - 1) * blocks)
        step_count = max(0, min(blocks, 2 - (hop_index - 1) * blocks))
        arrived = passed_along((block_keys, value_blocks, doc_float, block_steps), "ctx", hop_index)
        filler = jnp.broadcast_to(identity, (key_count - step_count, groups, head_size, head_size))
        received.insert(
            0,
            (
                arrived[0],
                arrived[1],
                arrived[2],
                jnp.concatenate([filler, arrived[3][key_count - step_count :]], axis=0),
            ),
        )
    ext_keys = jnp.concatenate([item[0] for item in received] + [block_keys], axis=0)
    ext_values = jnp.concatenate([item[1] for item in received] + [value_blocks], axis=0)
    ext_docs = jnp.concatenate([item[2] for item in received] + [doc_float], axis=0)
    ext_steps = jnp.concatenate([item[3] for item in received] + [block_steps], axis=0)
    score_scale = 1.0 / math.sqrt(head_size)
    causal = lax.broadcasted_iota(jnp.int32, (length, length), 0) >= lax.broadcasted_iota(
        jnp.int32, (length, length), 1
    )
    own_allowed = (document_blocks[:, None, :, None] == document_blocks[:, None, None, :]) & causal
    softmax_state = (
        jnp.full((blocks, groups, length, 1), -jnp.inf, jnp.float32),
        jnp.zeros((blocks, groups, length, 1), jnp.float32),
        jnp.zeros((blocks, groups, length, head_size), jnp.float32),
    )
    softmax_state = absorb(softmax_state, intra_scores * score_scale, own_allowed, value_blocks)
    current = block_queries
    anchor = lax.axis_index("ctx") * blocks
    block_ids = lax.iota(jnp.int32, blocks)
    for distance in range(1, 4):
        lowest = 3 - distance
        if distance > 1:
            current = contract(
                "bhie,bhef->bhif", current, ext_steps[lowest + 1 : lowest + 1 + blocks]
            )
        valid_block = anchor + block_ids - distance >= 0
        allowed = (
            doc_float[:, None, :, None] == ext_docs[lowest : lowest + blocks][:, None, None, :]
        ) & valid_block[:, None, None, None]
        raw_scores = (
            contract("bhid,bhjd->bhij", current, ext_keys[lowest : lowest + blocks]) * score_scale
        )
        softmax_state = absorb(
            softmax_state, raw_scores, allowed, ext_values[lowest : lowest + blocks]
        )
    attended = softmax_state[2] / softmax_state[1]
    flattened = jnp.transpose(attended, (0, 2, 1, 3)).reshape(token_rows, groups * head_size)
    share_rows = token_rows // lax.axis_size("head")
    partial_out = jnp.dot(
        flattened, out_weight, precision=HIGHEST, preferred_element_type=jnp.float32
    )
    full_sum = lax.psum(partial_out, "head")
    return lax.dynamic_slice_in_dim(full_sum, lax.axis_index("head") * share_rows, share_rows, 0)


def solution(mesh):
    return jax.shard_map(
        shards,
        mesh=mesh,
        in_specs=(
            P("ctx", "head"),
            P("ctx", "head"),
            P("ctx", "head"),
            P("ctx", "head"),
            P("head", "ctx"),
            P("ctx"),
            P("head", None),
        ),
        out_specs=P(("ctx", "head"), None),
        check_vma=False,
    )
```

profile of v0, /device:TPU:1, one launch (start us, length us, event | category | flops | bytes accessed | tf_op | source)
XLA Modules:
  0.0 695.9 jit_solution(2687625667432584392)
XLA Ops:
  7.8 4.5 collective-permute-start
  12.3 4.4 collective-permute-start.3
  16.7 4.4 collective-permute-start.7
  27.8 26.4 %copy.389 = f32[4,4,128,128]{1,3,2,0:T(8,128)} copy(f32[4,4,128,128]{2,3,1,0:T(8,128)S(1)} %fusion.52) | data formatting | bytes 2097152 | tf_op jit(solution)/shard_map/add | solution.py:71
  54.2 53.1 %reshape.1072 = f32[1,4,4,16,2,4,16,2,4]{5,4,3,8,7,6,2,1,0:T(2,128)} reshape(f32[4,4,128,128]{2,3,1,0:T(8,128)S(1)} %fusion.52) | data formatting | bytes 2097152 | tf_op jit(solution)/shard_map/reshape | solution.py:36
  107.3 26.6 %reshape.966 = f32[1,4,4,8,2,8,8,2,8]{5,4,3,8,7,6,2,1,0:T(2,128)} reshape(f32[4,4,128,128]{2,3,1,0:T(8,128)S(1)} %fusion.52) | data formatting | bytes 2097152 | tf_op jit(solution)/shard_map/reshape | solution.py:36
  133.9 12.1 %reshape.971 = f32[1,4,4,4,2,16,4,2,16]{5,4,3,8,7,6,2,1,0:T(2,128)} reshape(f32[4,4,128,128]{2,3,1,0:T(8,128)S(1)} %fusion.52) | data formatting | bytes 2097152 | tf_op jit(solution)/shard_map/reshape | solution.py:36
  146.1 4.6 reshape.976
  158.5 38.3 %copy.516 = f32[1,4,4,64,2,1,64,2,1]{2,1,6,3,7,4,8,5,0:T(4,128)} copy(f32[1,4,4,64,2,1,64,2,1]{2,7,6,4,3,1,8,5,0:T(2,128)} %bitcast.445) | data formatting | bytes 2097152 | tf_op jit(solution)/shard_map/reshape | solution.py:36
  202.0 38.3 %copy.515 = f32[1,4,4,32,2,2,32,2,2]{2,1,6,3,8,7,5,4,0:T(4,128)} copy(f32[1,4,4,32,2,2,32,2,2]{2,8,7,6,5,4,3,1,0:T(2,128)} %bitcast.446) | data formatting | bytes 2097152 | tf_op jit(solution)/shard_map/reshape | solution.py:36
  242.6 8.4 %copy.397 = f32[32,4,4,2,2,2,2]{6,4,0,2,1,5,3:T(2,128)} copy(f32[32,4,4,2,2,2,2]{2,1,6,5,4,3,0:T(4,128)S(1)} %gather_fusion.1) | data formatting | bytes 65536 | tf_op jit(solution)/shard_map/jit(diagonal)/gather | solution.py:37
  253.7 4.5 fusion.119
  263.9 104.7 %copy.402 = f32[1,4,4,16,2,4,16,2,4]{8,5,6,3,7,4,2,1,0:T(4,128)} copy(f32[1,4,4,16,2,4,16,2,4]{5,4,3,8,7,6,2,1,0:T(2,128)} %reshape.1072) | data formatting | bytes 2097152 | tf_op jit(solution)/shard_map/reshape | solution.py:36
  368.6 4.5 gather_fusion.2
  381.9 25.7 %copy.406 = f32[1,4,4,8,2,8,8,2,8]{8,5,6,3,7,4,2,1,0:T(8,128)} copy(f32[1,4,4,8,2,8,8,2,8]{5,4,3,8,7,6,2,1,0:T(2,128)} %reshape.966) | data formatting | bytes 2097152 | tf_op jit(solution)/shard_map/reshape | solution.py:36
  407.6 6.6 gather_fusion.3
  419.9 13.2 %copy.410 = f32[1,4,4,4,2,16,4,2,16]{8,5,6,3,7,4,2,1,0:T(8,128)} copy(f32[1,4,4,4,2,16,4,2,16]{5,4,3,8,7,6,2,1,0:T(2,128)} %reshape.971) | data formatting | bytes 2097152 | tf_op jit(solution)/shard_map/reshape | solution.py:36
  433.2 4.1 gather_fusion.4
  442.1 7.6 %copy.414 = f32[1,4,4,2,2,32,2,2,32]{8,5,6,3,7,4,2,1,0:T(8,128)} copy(f32[1,4,4,2,2,32,2,2,32]{5,4,3,8,7,6,2,1,0:T(2,128)} %reshape.976) | data formatting | bytes 2097152 | tf_op jit(solution)/shard_map/reshape | solution.py:36
  463.9 3.8 fusion.45
  519.1 3.7 collective-permute-start.9
  524.9 4.4 collective-permute-start.8
  530.6 3.9 collective-permute-start.6
  535.6 44.0 %collective-permute-start.10 = (f32[1,4,512,128]{2,3,1,0:T(8,128)}, f32[1,4,512,128]{2,3,1,0:T(8,128)S(1)}, u32[]{:S(2)}, u32[]{:S(2)}) collective-permute-start(f32[1,4,512,128]{2,3,1,0:T(8,128)} %bitcast.477), channel_id=1, source_target_pairs={{0,6},{2,8},{4,10},{6,12},{8,14},{10,16},{12,18},{14,20},{16,22},{... | collective-permute-start | bytes 3145736 | tf_op jit(solution)/shard_map/ppermute | solution.py:17
  582.5 5.3 fusion.13
  587.8 5.3 fusion.14
  593.1 4.1 fusion.15
  604.0 16.8 %collective-permute-done.10 = f32[1,4,512,128]{2,3,1,0:T(8,128)S(1)} collective-permute-done((f32[1,4,512,128]{2,3,1,0:T(8,128)}, f32[1,4,512,128]{2,3,1,0:T(8,128)S(1)}, u32[]{:S(2)}, u32[]{:S(2)}) %collective-permute-start.10) | collective-permute-done | bytes 1048608 | tf_op jit(solution)/shard_map/ppermute | solution.py:17
  624.4 5.2 fusion.59
  629.7 3.7 fusion.94
  633.4 8.6 %fusion.171 = f32[512,2048]{1,0:T(8,128)} fusion(f32[512,512]{0,1:T(8,128)S(1)} %bitcast.468, f32[512,2048]{1,0:T(8,128)S(1)} %copy-done.8), kind=kOutput, calls=%fused_computation.286 | convolution fusion | flops 6442450944 | bytes 9437184 | tf_op jit(solution)/shard_map/dot_general | solution.py:219
  642.0 43.7 %all-reduce.10.cloned.1.call-done = f32[512,2048]{1,0:T(8,128)} async-done(((f32[512,2048]{1,0:T(8,128)}), f32[512,2048]{1,0:T(8,128)}) %all-reduce.10.cloned.1.call-update) | async-done | bytes 4194320 | tf_op jit(solution)/shard_map/psum | solution.py:222
  (195 shorter events, 136.5 us)
Async XLA Ops:
  6.5 679.2 %all-reduce.10.cloned.1.call-start = ((), (), s32[]{:S(2)}) async-start(), calls=%async_computation | async-start | bytes 8388608 | tf_op jit(solution)/shard_map/psum | solution.py:222
  7.8 511.3 %collective-permute-start = (f32[1,512]{1,0:T(1,128)}, f32[1,512]{1,0:T(1,128)}, u32[]{:S(2)}, u32[]{:S(2)}) collective-permute-start(f32[1,512]{1,0:T(1,128)} %bitcast.134), channel_id=1, source_target_pairs={{0,2},{2,4},{4,6},{6,8},{8,10},{10,12},{12,14},{14,16},{16,18},{18... | collective-permute-start | bytes 6152 | tf_op jit(solution)/shard_map/ppermute | solution.py:17
  12.3 510.4 %collective-permute-start.3 = (f32[1,512]{1,0:T(1,128)}, f32[1,512]{1,0:T(1,128)}, u32[]{:S(2)}, u32[]{:S(2)}) collective-permute-start(f32[1,512]{1,0:T(1,128)} %bitcast.134), channel_id=1, source_target_pairs={{0,4},{2,6},{4,8},{6,10},{8,12},{10,14},{12,16},{14,18},{16,20},{1... | collective-permute-start | bytes 6152 | tf_op jit(solution)/shard_map/ppermute | solution.py:17
  16.7 508.2 %collective-permute-start.7 = (f32[1,512]{1,0:T(1,128)}, f32[1,512]{1,0:T(1,128)}, u32[]{:S(2)}, u32[]{:S(2)}) collective-permute-start(f32[1,512]{1,0:T(1,128)} %bitcast.134), channel_id=1, source_target_pairs={{0,6},{2,8},{4,10},{6,12},{8,14},{10,16},{12,18},{14,20},{16,22},{... | collective-permute-start | bytes 6152 | tf_op jit(solution)/shard_map/ppermute | solution.py:17
  22.9 3.1 copy-start.27
  146.1 7.2 %copy-start = (f32[512,512]{1,0:T(8,128)S(1)}, f32[512,512]{1,0:T(8,128)}, u32[]{:S(2)}) copy-start(f32[512,512]{1,0:T(8,128)} %param.10) | copy-start | bytes 3145732
  153.2 3.8 copy-start.9
  158.5 40.5 %copy-start.29 = (f32[1,4,4,64,1,2]{3,2,1,5,4,0:T(4,128)S(1)}, f32[1,4,4,64,1,2]{3,2,1,5,4,0:T(4,128)}, u32[]{:S(2)}) copy-start(f32[1,4,4,64,1,2]{3,2,1,5,4,0:T(4,128)} %constant.40.clone.1) | copy-start | bytes 24580
  457.4 3.9 copy-start.5
  457.7 5.8 copy-start.10
  463.9 5.6 copy-start.11
  469.6 6.1 copy-start.1
  471.6 5.9 copy-start.3
  477.5 103.2 %collective-permute-start.1 = (f32[1,4,512,128]{3,2,1,0:T(8,128)}, f32[1,4,512,128]{3,2,1,0:T(8,128)}, u32[]{:S(2)}, u32[]{:S(2)}) collective-permute-start(f32[1,4,512,128]{3,2,1,0:T(8,128)} %bitcast.148), channel_id=1, source_target_pairs={{0,2},{2,4},{4,6},{6,8},{8,10},{10,12},{12,14},{14,16},{16,18},{18... | collective-permute-start | bytes 3145736 | tf_op jit(solution)/shard_map/ppermute | solution.py:17
  480.7 107.1 %collective-permute-start.5 = (f32[1,4,512,128]{3,2,1,0:T(8,128)}, f32[1,4,512,128]{3,2,1,0:T(8,128)}, u32[]{:S(2)}, u32[]{:S(2)}) collective-permute-start(f32[1,4,512,128]{3,2,1,0:T(8,128)} %bitcast.148), channel_id=1, source_target_pairs={{0,4},{2,6},{4,8},{6,10},{8,12},{10,14},{12,16},{14,18},{16,20},{1... | collective-permute-start | bytes 3145736 | tf_op jit(solution)/shard_map/ppermute | solution.py:17
  489.0 6.5 copy-start.4
  489.0 7.2 %copy-start.2 = (f32[1,4,4,128,128]{3,4,2,1,0:T(8,128)S(1)}, f32[1,4,4,128,128]{3,4,2,1,0:T(8,128)}, u32[]{:S(2)}) copy-start(f32[1,4,4,128,128]{3,4,2,1,0:T(8,128)} %copy-done.1) | copy-start | bytes 3145732
  492.2 8.0 %copy-start.6 = (f32[4,128,4,128]{3,2,1,0:T(4,128)S(1)}, f32[4,128,4,128]{3,2,1,0:T(4,128)}, u32[]{:S(2)}) copy-start(f32[4,128,4,128]{3,2,1,0:T(4,128)} %reshape.949) | copy-start | bytes 3145732
  492.2 8.0 %copy-start.7 = (f32[4,128,4,128]{3,2,1,0:T(4,128)S(1)}, f32[4,128,4,128]{3,2,1,0:T(4,128)}, u32[]{:S(2)}) copy-start(f32[4,128,4,128]{3,2,1,0:T(4,128)} %reshape.948) | copy-start | bytes 3145732
  495.6 7.0 %copy-start.28 = (s32[512]{0:T(512)S(1)}, s32[512]{0:T(512)}, u32[]{:S(2)}) copy-start(s32[512]{0:T(512)} %param.12) | copy-start | bytes 6148
  519.1 61.6 %copy-start.26 = (f32[512,512]{0,1:T(8,128)S(1)}, f32[512,512]{0,1:T(8,128)}, u32[]{:S(2)}) copy-start(f32[512,512]{0,1:T(8,128)} %copy.433) | copy-start | bytes 3145732
  519.1 74.0 %collective-permute-start.9 = (f32[1,4,512,128]{3,2,1,0:T(8,128)}, f32[1,4,512,128]{3,2,1,0:T(8,128)S(1)}, u32[]{:S(2)}, u32[]{:S(2)}) collective-permute-start(f32[1,4,512,128]{3,2,1,0:T(8,128)} %bitcast.148), channel_id=1, source_target_pairs={{0,6},{2,8},{4,10},{6,12},{8,14},{10,16},{12,18},{14,20},{16,22},{... | collective-permute-start | bytes 3145736 | tf_op jit(solution)/shard_map/ppermute | solution.py:17
  522.7 7.9 %collective-permute-start.4 = (f32[1,4,128,128]{3,2,1,0:T(8,128)S(1)}, f32[1,4,128,128]{3,2,1,0:T(8,128)S(1)}, u32[]{:S(2)}, u32[]{:S(2)}) collective-permute-start(f32[1,4,128,128]{3,2,1,0:T(8,128)S(1)} %convolution_bitcast_fusion.3), channel_id=1, source_target_pairs={{0,2},{2,4},{4,6},{6,8},{8,10},{10,12},{12,14},{14,16},{16,18},{18... | collective-permute-start | bytes 786440 | tf_op jit(solution)/shard_map/ppermute | solution.py:17
  524.9 10.7 %collective-permute-start.8 = (f32[1,4,128,128]{3,2,1,0:T(8,128)S(1)}, f32[1,4,128,128]{3,2,1,0:T(8,128)S(1)}, u32[]{:S(2)}, u32[]{:S(2)}) collective-permute-start(f32[1,4,128,128]{3,2,1,0:T(8,128)S(1)} %convolution_bitcast_fusion.3), channel_id=1, source_target_pairs={{0,4},{2,6},{4,8},{6,10},{8,12},{10,14},{12,16},{14,18},{16,20},{1... | collective-permute-start | bytes 786440 | tf_op jit(solution)/shard_map/ppermute | solution.py:17
  530.6 69.7 %collective-permute-start.6 = (f32[1,4,512,128]{2,3,1,0:T(8,128)}, f32[1,4,512,128]{2,3,1,0:T(8,128)S(1)}, u32[]{:S(2)}, u32[]{:S(2)}) collective-permute-start(f32[1,4,512,128]{2,3,1,0:T(8,128)} %bitcast.476), channel_id=1, source_target_pairs={{0,4},{2,6},{4,8},{6,10},{8,12},{10,14},{12,16},{14,18},{16,20},{1... | collective-permute-start | bytes 3145736 | tf_op jit(solution)/shard_map/ppermute | solution.py:17
  535.6 85.2 %collective-permute-start.10 = (f32[1,4,512,128]{2,3,1,0:T(8,128)}, f32[1,4,512,128]{2,3,1,0:T(8,128)S(1)}, u32[]{:S(2)}, u32[]{:S(2)}) collective-permute-start(f32[1,4,512,128]{2,3,1,0:T(8,128)} %bitcast.477), channel_id=1, source_target_pairs={{0,6},{2,8},{4,10},{6,12},{8,14},{10,16},{12,18},{14,20},{16,22},{... | collective-permute-start | bytes 3145736 | tf_op jit(solution)/shard_map/ppermute | solution.py:17
  580.7 49.0 %collective-permute-start.2 = (f32[1,4,512,128]{2,3,1,0:T(8,128)S(1)}, f32[1,4,512,128]{2,3,1,0:T(8,128)S(1)}, u32[]{:S(2)}, u32[]{:S(2)}) collective-permute-start(f32[1,4,512,128]{2,3,1,0:T(8,128)S(1)} %bitcast.478), channel_id=1, source_target_pairs={{0,2},{2,4},{4,6},{6,8},{8,10},{10,12},{12,14},{14,16},{16,18},{18... | collective-permute-start | bytes 3145736 | tf_op jit(solution)/shard_map/ppermute | solution.py:17
  604.0 20.4 %copy-start.22 = (f32[4,128,512]{1,2,0:T(8,128)S(1)}, f32[4,128,512]{1,2,0:T(8,128)}, u32[]{:S(2)}) copy-start(f32[4,128,512]{1,2,0:T(8,128)} %get-tuple-element.30) | copy-start | bytes 3145732
  604.0 20.4 %copy-start.23 = (f32[4,128,512]{1,2,0:T(8,128)S(1)}, f32[4,128,512]{1,2,0:T(8,128)}, u32[]{:S(2)}) copy-start(f32[4,128,512]{1,2,0:T(8,128)} %maximum_bitcast_fusion.4) | copy-start | bytes 3145732
  604.0 20.4 %copy-start.24 = (f32[4,128,512]{1,2,0:T(8,128)S(1)}, f32[4,128,512]{1,2,0:T(8,128)}, u32[]{:S(2)}) copy-start(f32[4,128,512]{1,2,0:T(8,128)} %maximum_bitcast_fusion.5) | copy-start | bytes 3145732
  604.0 20.4 %copy-start.25 = (f32[4,128,512]{1,2,0:T(8,128)S(1)}, f32[4,128,512]{1,2,0:T(8,128)}, u32[]{:S(2)}) copy-start(f32[4,128,512]{1,2,0:T(8,128)} %maximum_bitcast_fusion.6) | copy-start | bytes 3145732
  629.7 3.7 copy-start.8
  (10 other events, 12.4 us)
Sparse Core Ops, SparseCore 0:
  642.1 43.5 all-reduce.9
where the time goes:
time: 702 us; the launch traced here: 696 us
  local copies, waits for them, and re-layouts  424 us (60%)
  matrix products  98.2 us (14%)
  starting transfers between devices  79.6 us (11%)
  waiting for transfers between devices  60.6 us (9%)
  other arithmetic  18.3 us (3%)
  between operations  14.8 us (2%)
    reshape x10, local copies, waits for them, and re-layouts, unit_lower_inverse(): tiled = lower_mat.reshape(lead + (count, 2, size, count, 2, size))  324 us
    dot_general x50, matrix products, contract(): return jnp.einsum(pattern, left_operand, right_operand, precision=HIGHEST)  89.6 us
    ppermute x11, starting transfers between devices, passed_along(): lax.ppermute(value, axis, [(source, source + steps) for source in range(l...  79.6 us
    psum x1, waiting for transfers between devices, shards(): full_sum = lax.psum(partial_out, 'head')  43.7 us
    gather x13, local copies, waits for them, and re-layouts, unit_lower_inverse(): diagonal_tiles = jnp.diagonal(tiled, axis1=depth, axis2=depth + 3)  36.4 us
    add x1, local copies, waits for them, and re-layouts, local_parts(): jnp.eye(piece_size, dtype=jnp.float32)  26.4 us
    ppermute x11, waiting for transfers between devices, passed_along(): lax.ppermute(value, axis, [(source, source + steps) for source in range(l...  16.9 us
  transfers between devices with their start and end apart: 12, of which 2 were waited for; matrix products, arithmetic and copies ran while one was open for 75% of the time, Pallas kernels for 0%

commit v1 on v0

v1 whole, which is shorter than its diff:
```python
import functools
import math

import jax
import jax.numpy as jnp
from jax import lax
from jax.experimental import pallas as pl
from jax.experimental.pallas import tpu as pltpu
from jax.sharding import PartitionSpec as P

MESH = pl.DeviceIdType.MESH
HIGH = lax.Precision.HIGH
ROWS = 512
DH = 128
G = 4
PIECE = 128
PIECES = ROWS // PIECE
MASKED = -1e30


def dot(left, right, left_dim=1, right_dim=0):
    return lax.dot_general(
        left,
        right,
        (((left_dim,), (right_dim,)), ((), ())),
        precision=HIGH,
        preferred_element_type=jnp.float32,
    )


def iotas(rows, columns):
    return (
        lax.broadcasted_iota(jnp.int32, (rows, columns), 0),
        lax.broadcasted_iota(jnp.int32, (rows, columns), 1),
    )


def unit_lower_inverses(lowers):
    row, col = iotas(PIECE, PIECE)
    eye = jnp.where(row == col, 1.0, 0.0)

    def level_part(lower, bit):
        keep = ((row >> (bit + 1)) == (col >> (bit + 1))) & (((row >> bit) & 1) == 1) & (((col >> bit) & 1) == 0)
        return jnp.where(keep, lower, 0.0)

    inverses = [eye - level_part(lower, 0) for lower in lowers]
    for bit in range(1, 7):
        products = [dot(level_part(lower, bit), inverse) for lower, inverse in zip(lowers, inverses)]
        products = [dot(inverse, product) for inverse, product in zip(inverses, products)]
        inverses = [inverse - product for inverse, product in zip(inverses, products)]
    return inverses


def local_forms(query, key, trans, beta):
    row, col = iotas(PIECE, PIECE)
    eye = jnp.where(row == col, 1.0, 0.0)
    unit = trans * lax.rsqrt(jnp.sum(trans * trans, axis=-1, keepdims=True) + 1e-06)
    beta_unit = unit * beta
    pieces = [slice(p * PIECE, (p + 1) * PIECE) for p in range(PIECES)]
    units = [unit[p] for p in pieces]
    beta_units = [beta_unit[p] for p in pieces]
    queries = [query[p] for p in pieces]
    keys = [key[p] for p in pieces]
    products = [
        dot(jnp.concatenate([b, q], axis=0), jnp.concatenate([u, k], axis=0), 1, 1)
        for b, q, u, k in zip(beta_units, queries, units, keys)
    ]
    lowers = [jnp.where(row > col, x[:PIECE, :PIECE], 0.0) for x in products]
    beta_keys = [jnp.where(row > col, x[:PIECE, PIECE:], 0.0) for x in products]
    query_dirs = [jnp.where(row >= col, x[PIECE:, :PIECE], 0.0) for x in products]
    inverses = unit_lower_inverses(lowers)
    solved = [dot(i, jnp.concatenate([bk, bu], axis=1)) for i, bk, bu in zip(inverses, beta_keys, beta_units)]
    taken = [dot(d, s) for d, s in zip(query_dirs, solved)]
    own_scores = [x[PIECE:, PIECE:] - y[:, :PIECE] for x, y in zip(products, taken)]
    query_hats = [q - y[:, PIECE:] for q, y in zip(queries, taken)]
    backs = [dot(s, u, 0, 0) for s, u in zip(solved, units)]
    key_hats = [k - z[:PIECE] for k, z in zip(keys, backs)]
    steps_t = [eye - z[PIECE:] for z in backs]
    return query_hats, key_hats, own_scores, steps_t


def kernel(
    n,
    q_hbm, k_hbm, v_hbm, t_hbm, beta_ref, doc_ref, w_hbm,
    out_ref,
    q_in, k_in, t_in, v_in, flat, cols, doc_own,
    scores, ks_send, q_send,
    v_all, ks_all, q_all, doc_all,
    own_o, own_m, own_l,
    cross_o, cross_st, ret_o, ret_st,
    att, att_got, w_own, w_got,
    in_sem, v_ssem, v_rsem, ks_ssem, ks_rsem, q_ssem, q_rsem, d_ssem, d_rsem,
    vz_ssem, kz_ssem, dz_ssem, o_ssem, o_rsem, s_ssem, s_rsem, w_sem, a_sem,
):
    me = lax.axis_index("ctx")
    core = lax.axis_index("head")
    x = lax.rem(me, G)
    row_start = me - x
    up = lax.rem(me + G, n)
    down = lax.rem(me + n - G, n)
    half = ROWS // 2

    def ring(off):
        return lax.rem(x + off, G)

    def remote(src, dst, ssem, rsem, ctx=None, head=None):
        device = {"ctx": me if ctx is None else ctx, "head": core if head is None else head}
        return pltpu.make_async_remote_copy(
            src_ref=src, dst_ref=dst, send_sem=ssem, recv_sem=rsem, device_id=device, device_id_type=MESH
        )

    def head_cols(h):
        return pl.ds(pl.multiple_of(h * DH, DH), DH)

    def load(i, src, dst, h):
        return pltpu.make_async_copy(src.at[:, head_cols(h)], dst.at[h], in_sem.at[i, h])

    loads = ((k_hbm, k_in), (t_hbm, t_in), (q_hbm, q_in), (v_hbm, v_in))
    for off in (3, 2, 1, 0):
        for i in range(3):
            load(i, *loads[i], ring(off)).start()
    for off in (0, 1, 2, 3):
        load(3, *loads[3], ring(off)).start()
    own_w = pltpu.make_async_copy(w_hbm, w_own, w_sem.at[0])

    barrier = pltpu.get_barrier_semaphore()
    for off in (1, 2, 3):
        pl.semaphore_signal(barrier, inc=1, device_id={"ctx": row_start + ring(off), "head": core}, device_id_type=MESH)
    for ctx in (up, down):
        pl.semaphore_signal(barrier, inc=1, device_id={"ctx": ctx, "head": core}, device_id_type=MESH)
    pl.semaphore_signal(barrier, inc=1, device_id={"ctx": me, "head": 1 - core}, device_id_type=MESH)
    pl.semaphore_wait(barrier, 6)

    def v_copy(off):
        h = ring(off)
        return remote(v_hbm.at[:, head_cols(h)], v_all.at[3 + x], v_ssem.at[off], v_rsem.at[3 + x], row_start + h)

    def doc_copy(off):
        return remote(doc_own, doc_all.at[3 + x], d_ssem.at[off], d_rsem.at[3 + x], row_start + ring(off))

    def ks_copy(off):
        h = ring(off)
        return remote(ks_send.at[h], ks_all.at[3 + x], ks_ssem.at[off], ks_rsem.at[3 + x], row_start + h)

    def q_copy(off):
        h = ring(off)
        return remote(q_send.at[h], q_all.at[x], q_ssem.at[off], q_rsem.at[x], row_start + h)

    def from_slot(ref, ssem, rsem, slot):
        return remote(ref.at[slot], ref.at[slot], ssem.at[0], rsem.at[slot], row_start)

    def up_copy(ref, ssem, rsem, b):
        return remote(ref.at[3 + b], ref.at[b - 1], ssem.at[b - 1], rsem.at[b - 1], up)

    w_copy = remote(w_hbm, w_got, w_sem.at[1], w_sem.at[2], None, 1 - core)
    for off in (2, 1, 3):
        v_copy(off).start()
    own_w.start()
    w_copy.start()

    doc_row = doc_ref[...].astype(jnp.float32)
    doc_own[...] = jnp.broadcast_to(doc_row, (8, ROWS))
    flat[...] = jnp.zeros_like(flat)
    flat[0:G, :] = beta_ref[...]
    flat[8:16, :] = jnp.broadcast_to(doc_row, (8, ROWS))
    cols[...] = jnp.transpose(flat[...])
    doc_all[pl.ds(3 + x, 1)] = jnp.broadcast_to(doc_row, (8, ROWS))[None]
    for off in (1, 2, 3):
        doc_copy(off).start()

    lane = lax.broadcasted_iota(jnp.int32, (ROWS, DH), 1)

    @pl.loop(0, G)
    def _(it):
        off = G - 1 - it
        h = ring(off)
        for i in range(3):
            load(i, *loads[i], h).wait()
        beta = jnp.sum(jnp.where(lane == h, cols[...], 0.0), axis=1, keepdims=True)
        query = q_in[h] * (math.log2(math.e) / math.sqrt(DH))
        query_hats, key_hats, own_scores, steps_t = local_forms(query, k_in[h], t_in[h], beta)
        carried = key_hats[0]
        prefix_t = steps_t[0]
        q_send[h, 0:PIECE] = query_hats[0]
        scores[h, 0:PIECE, 0:PIECE] = own_scores[0]
        for p in range(1, PIECES):
            here = slice(p * PIECE, (p + 1) * PIECE)
            scores[h, here, 0 : p * PIECE] = dot(query_hats[p], carried, 1, 1)
            scores[h, here, here] = own_scores[p]
            carried = jnp.concatenate([dot(carried, steps_t[p]), key_hats[p]], axis=0)
            q_send[h, here] = dot(query_hats[p], prefix_t, 1, 1)
            prefix_t = dot(prefix_t, steps_t[p])
        ks_send[h, 0:ROWS] = carried
        ks_send[h, ROWS : ROWS + DH] = prefix_t

        @pl.when(it < G - 1)
        def _():
            ks_copy(off).start()
            q_copy(off).start()

    load(3, *loads[3], x).wait()
    v_all[pl.ds(3 + x, 1)] = v_in[pl.ds(x, 1)]
    ks_all[pl.ds(3 + x, 1)] = ks_send[pl.ds(x, 1)]
    q_all[pl.ds(x, 1)] = q_send[pl.ds(x, 1)]

    for b in (3, 2, 1):
        @pl.when(x != b)
        def _():
            from_slot(v_all, v_ssem, v_rsem, 3 + b).wait_recv()
            from_slot(doc_all, d_ssem, d_rsem, 3 + b).wait_recv()
        up_copy(v_all, vz_ssem, v_rsem, b).start()
        up_copy(doc_all, dz_ssem, d_rsem, b).start()
    for b in (3, 2, 1):
        @pl.when(x != b)
        def _():
            from_slot(ks_all, ks_ssem, ks_rsem, 3 + b).wait_recv()
        up_copy(ks_all, kz_ssem, ks_rsem, b).start()

    for off in (1, 2, 3):
        load(3, *loads[3], ring(off)).wait()
    row, col = iotas(PIECE, PIECE)

    @pl.loop(0, G)
    def _(h):
        for p in range(PIECES):
            here = slice(p * PIECE, (p + 1) * PIECE)
            width = (p + 1) * PIECE
            raw = scores[h, here, 0:width]
            same = cols[here, 8:9] == doc_own[0:1, 0:width]
            wide_row, wide_col = iotas(PIECE, width)
            allowed = same & (wide_row + p * PIECE >= wide_col)
            masked = jnp.where(allowed, raw, MASKED)
            peak = jnp.max(masked, axis=-1, keepdims=True)
            weights = jnp.exp2(masked - peak)
            own_m[h, here] = peak
            own_l[h, here] = jnp.sum(weights, axis=-1, keepdims=True)
            own_o[h, here] = dot(weights, v_in[h, 0:width])

    b0 = (0,)
    @pl.when(x != 0)
    def _():
        from_slot(v_all, v_ssem, v_rsem, 3).wait_recv()
        from_slot(doc_all, d_ssem, d_rsem, 3).wait_recv()
        from_slot(ks_all, ks_ssem, ks_rsem, 3).wait_recv()

    def o_copy(b, slot):
        return remote(cross_o.at[b], ret_o.at[slot], o_ssem.at[b], o_rsem.at[slot], row_start + b)

    def st_copy(b, slot):
        return remote(cross_st.at[b], ret_st.at[slot], s_ssem.at[b], s_rsem.at[slot], row_start + b)

    for b in (3, 2, 1, 0):
        slot = 3 + b

        @pl.when(x != b)
        def _():
            from_slot(q_all, q_ssem, q_rsem, b).wait_recv()

        if b < 3:
            halo = b
            up_copy(v_all, vz_ssem, v_rsem, halo + 1).wait_recv()
            up_copy(doc_all, dz_ssem, d_rsem, halo + 1).wait_recv()
            up_copy(ks_all, kz_ssem, ks_rsem, halo + 1).wait_recv()
        flat[0:8, :] = doc_all[slot]
        doc_col = jnp.transpose(flat[...])[:, 0:1]
        key_docs = []
        for d in (1, 2, 3):
            key_doc = doc_all[slot - d, 0:1, :]
            if slot - d < 3:
                key_doc = jnp.where(me >= G, key_doc, -1.0)
            key_docs.append(key_doc)
        current = q_all[b]
        raws = []
        for d in (1, 2, 3):
            if d > 1:
                current = dot(current, ks_all[slot - d + 1, ROWS : ROWS + DH], 1, 1)
            raw = dot(current, ks_all[slot - d, 0:ROWS], 1, 1)
            raws.append(jnp.where(doc_col == key_docs[d - 1], raw, MASKED))
        peak = functools.reduce(jnp.maximum, [jnp.max(r, axis=-1, keepdims=True) for r in raws])
        total = jnp.zeros((ROWS, 1), jnp.float32)
        summed = jnp.zeros((ROWS, DH), jnp.float32)
        for d in (1, 2, 3):
            weights = jnp.exp2(raws[d - 1] - peak)
            total = total + jnp.sum(weights, axis=-1, keepdims=True)
            summed = summed + dot(weights, v_all[slot - d])
        cross_o[b] = summed
        stats = jnp.where(lane == 0, peak, jnp.where(lane == 1, total, 0.0))
        cross_st[b] = jnp.transpose(stats)[0:8, :]

        @pl.when(x != b)
        def _():
            o_copy(b, x).start()
            st_copy(b, x).start()

        @pl.when(x == b)
        def _():
            ret_o[pl.ds(x, 1)] = cross_o[b][None]
            ret_st[pl.ds(x, 1)] = cross_st[b][None]

    for off in (1, 2, 3):
        h = ring(off)
        remote(ret_o.at[h], ret_o.at[h], o_ssem.at[0], o_rsem.at[h], row_start).wait_recv()
        remote(ret_st.at[h], ret_st.at[h], s_ssem.at[0], s_rsem.at[h], row_start).wait_recv()
    for h in range(G):
        flat[8 * h : 8 * h + 8, :] = ret_st[h]
    stat_cols = jnp.transpose(flat[...])
    for h in range(G):
        other_m = stat_cols[:, 8 * h : 8 * h + 1]
        other_l = stat_cols[:, 8 * h + 1 : 8 * h + 2]
        peak = jnp.maximum(own_m[h], other_m)
        mine = jnp.exp2(own_m[h] - peak)
        other = jnp.exp2(other_m - peak)
        total = mine * own_l[h] + other * other_l
        att[:, h * DH : (h + 1) * DH] = (mine * own_o[h] + other * ret_o[h]) / total

    mine_rows = pl.ds(pl.multiple_of(core * half, half), half)
    other_rows = pl.ds(pl.multiple_of((1 - core) * half, half), half)
    a_copy = remote(att.at[other_rows], att_got, a_sem.at[0], a_sem.at[1], None, 1 - core)
    a_copy.start()
    own_w.wait()
    tile = 512
    for j in range(4):
        at = slice(j * tile, (j + 1) * tile)
        out_ref[:, at] = dot(att[mine_rows, :], w_own[:, at])
    w_copy.wait()
    a_copy.wait()
    for j in range(4):
        at = slice(j * tile, (j + 1) * tile)
        out_ref[:, at] = out_ref[:, at] + dot(att_got[...], w_got[:, at])

    for off in (1, 2, 3):
        v_copy(off).wait_send()
        doc_copy(off).wait_send()
        ks_copy(off).wait_send()
        q_copy(off).wait_send()
    for b in (1, 2, 3):
        up_copy(v_all, vz_ssem, v_rsem, b).wait_send()
        up_copy(doc_all, dz_ssem, d_rsem, b).wait_send()
        up_copy(ks_all, kz_ssem, ks_rsem, b).wait_send()
    for b in range(G):
        @pl.when(x != b)
        def _():
            o_copy(b, x).wait_send()
            st_copy(b, x).wait_send()


def shards(n, queries, keys, values, transitions, betas, documents, out_weight):
    f32 = jnp.float32
    dma = pltpu.SemaphoreType.DMA
    columns = out_weight.shape[1]
    hbm = pl.BlockSpec(memory_space=pl.ANY)
    vmem = pl.BlockSpec(memory_space=pltpu.VMEM)
    heads = pltpu.VMEM((G, ROWS, DH), f32)
    return pl.pallas_call(
        functools.partial(kernel, n),
        out_shape=jax.ShapeDtypeStruct((ROWS // 2, columns), f32),
        in_specs=[hbm, hbm, hbm, hbm, vmem, vmem, hbm],
        out_specs=vmem,
        scratch_shapes=[
            heads, heads, heads, heads,
            pltpu.VMEM((DH, ROWS), f32), pltpu.VMEM((ROWS, DH), f32), pltpu.VMEM((8, ROWS), f32),
            pltpu.VMEM((G, ROWS, ROWS), f32), pltpu.VMEM((G, ROWS + DH, DH), f32), heads,
            pltpu.VMEM((7, ROWS, DH), f32), pltpu.VMEM((7, ROWS + DH, DH), f32), heads, pltpu.VMEM((7, 8, ROWS), f32),
            heads, pltpu.VMEM((G, ROWS, 1), f32), pltpu.VMEM((G, ROWS, 1), f32),
            heads, pltpu.VMEM((G, 8, ROWS), f32), heads, pltpu.VMEM((G, 8, ROWS), f32),
            pltpu.VMEM((ROWS, G * DH), f32), pltpu.VMEM((ROWS // 2, G * DH), f32),
            pltpu.VMEM((G * DH, columns), f32), pltpu.VMEM((G * DH, columns), f32),
            dma((4, G)), dma((4,)), dma((7,)), dma((4,)), dma((7,)), dma((4,)), dma((4,)), dma((4,)), dma((7,)),
            dma((3,)), dma((3,)), dma((3,)), dma((4,)), dma((4,)), dma((4,)), dma((4,)), dma((3,)), dma((2,)),
        ],
        compiler_params=pltpu.CompilerParams(
            collective_id=0, has_side_effects=True, vmem_limit_bytes=60 * 2**20
        ),
        name="path_layer",
    )(queries, keys, values, transitions, betas, documents.reshape(1, ROWS), out_weight)


def solution(mesh):
    return jax.shard_map(
        functools.partial(shards, mesh.shape["ctx"]),
        mesh=mesh,
        in_specs=(
            P("ctx", "head"),
            P("ctx", "head"),
            P("ctx", "head"),
            P("ctx", "head"),
            P("head", "ctx"),
            P("ctx"),
            P("head", None),
        ),
        out_specs=P(("ctx", "head"), None),
        check_vma=False,
    )
```

time: 702 us -> 99.6 us (0.14)
  local copies, waits for them, and re-layouts: 424 us -> 3.14 us
  matrix products: 98.2 us -> 0 us
  Pallas kernels: 0 us -> 96.2 us
  starting transfers between devices: 79.6 us -> 0 us
  waiting for transfers between devices: 60.6 us -> 0 us
  other arithmetic: 18.3 us -> 0 us
  between operations: 14.8 us -> 0.01 us
    reshape x14 -> x0, local copies, waits for them, and re-layouts: 328 us -> none  [the longest x10 324 us: unit_lower_inverse(): tiled = lower_mat.reshape(lead + (count, 2, size, count, 2, size))]
    dot_general x51 -> x0, matrix products: 98.2 us -> none  [the longest x50 89.6 us: contract(): return jnp.einsum(pattern, left_operand, right_operand, precision=HIGHEST)]
    pallas_call x0 -> x1, Pallas kernels: none -> 96.2 us  [shards(): pl.pallas_call(functools.partial(kernel, n), out_shape=jax.ShapeDtypeStru...]
    ppermute x11 -> x0, starting transfers between devices: 79.6 us -> none  [passed_along(): lax.ppermute(value, axis, [(source, source + steps) for source in range(l...]
    psum x1 -> x0, waiting for transfers between devices: 43.7 us -> none  [shards(): full_sum = lax.psum(partial_out, 'head')]
    gather x13 -> x0, local copies, waits for them, and re-layouts: 36.4 us -> none  [unit_lower_inverse(): diagonal_tiles = jnp.diagonal(tiled, axis1=depth, axis2=depth + 3)]
    add x1 -> x0, local copies, waits for them, and re-layouts: 26.4 us -> none  [local_parts(): jnp.eye(piece_size, dtype=jnp.float32)]
    ppermute x11 -> x0, waiting for transfers between devices: 16.9 us -> none  [passed_along(): lax.ppermute(value, axis, [(source, source + steps) for source in range(l...]
  transfers between devices with their start and end apart: 12 -> 0, of which waited for: 2 -> 0; matrix products, arithmetic and copies ran while one was open for 75% -> 0% of each run, Pallas kernels for 0% -> 0%
where the time goes in v1:
time: 99.6 us; the launch traced here: 99.4 us
  Pallas kernels  96.2 us (97%)
  local copies, waits for them, and re-layouts  3.14 us (3%)
    pallas_call x1, Pallas kernels, shards(): pl.pallas_call(functools.partial(kernel, n), out_shape=jax.ShapeDtypeStru...  96.2 us
    unnamed x1, local copies, waits for them, and re-layouts  3.14 us

profile of v1, /device:TPU:1, one launch (start us, length us, event | category | flops | bytes accessed | tf_op | source)
XLA Modules:
  0.0 99.4 jit_solution(6706988991130271758)
XLA Ops:
  0.0 96.2 %path_layer.1 = f32[256,2048]{1,0:T(8,128)} custom-call(f32[512,512]{1,0:T(8,128)} %q_hbm.1, f32[512,512]{1,0:T(8,128)} %k_hbm.1, f32[512,512]{1,0:T(8,128)} %v_hbm.1, f32[512,512]{1,0:T(8,128)} %t_hbm.1, f32[4,512]{1,0:T(4,128)} %beta_ref.1, s32[1,512]{1,0:T(1,128)} %bitcast.1, f32[512,2048]{1,0:T(8,128)} %w_hbm.1), custom_call_target="tpu_custom_call" | custom-call | tf_op jit(solution)/shard_map/path_layer/pallas_call | solution.py:354
  96.2 3.1 %copy.9 = f32[256,2048]{1,0:T(8,128)} copy(f32[256,2048]{1,0:T(8,128)} %path_layer.1) | data formatting | bytes 4194304

commit v2 on v1

--- a/solution.py
+++ b/solution.py
@@ -25,6 +25,17 @@
         (((left_dim,), (right_dim,)), ((), ())),
         precision=HIGH,
         preferred_element_type=jnp.float32,
+    )
+
+
+def split(value):
+    high = value.astype(jnp.bfloat16)
+    return high, (value - high.astype(jnp.float32)).astype(jnp.bfloat16)
+
+
+def half_dot(left, right, left_dim=1, right_dim=0):
+    return lax.dot_general(
+        left, right, (((left_dim,), (right_dim,)), ((), ())), preferred_element_type=jnp.float32
     )
 
 
@@ -83,12 +94,12 @@
     n,
     q_hbm, k_hbm, v_hbm, t_hbm, beta_ref, doc_ref, w_hbm,
     out_ref,
-    q_in, k_in, t_in, v_in, flat, cols, doc_own,
+    q_in, k_in, t_in, v_in, flat, cols, doc_own, doc_cols,
     scores, ks_send, q_send,
     v_all, ks_all, q_all, doc_all,
     own_o, own_m, own_l,
     cross_o, cross_st, ret_o, ret_st,
-    att, att_got, w_own, w_got,
+    att, att_got, w_own, w_got, w_high, w_low, kb, vb, qb,
     in_sem, v_ssem, v_rsem, ks_ssem, ks_rsem, q_ssem, q_rsem, d_ssem, d_rsem,
     vz_ssem, kz_ssem, dz_ssem, o_ssem, o_rsem, s_ssem, s_rsem, w_sem, a_sem,
 ):
@@ -123,12 +134,19 @@
         load(3, *loads[3], ring(off)).start()
     own_w = pltpu.make_async_copy(w_hbm, w_own, w_sem.at[0])
 
+    doc_row = doc_ref[...].astype(jnp.float32)
+    doc_own[...] = jnp.broadcast_to(doc_row, (8, ROWS))
+    doc_all[pl.ds(3 + x, 1)] = jnp.broadcast_to(doc_row, (8, ROWS))[None]
+    flat[...] = jnp.zeros_like(flat)
+    flat[0:G, :] = beta_ref[...]
     barrier = pltpu.get_barrier_semaphore()
     for off in (1, 2, 3):
         pl.semaphore_signal(barrier, inc=1, device_id={"ctx": row_start + ring(off), "head": core}, device_id_type=MESH)
     for ctx in (up, down):
         pl.semaphore_signal(barrier, inc=1, device_id={"ctx": ctx, "head": core}, device_id_type=MESH)
     pl.semaphore_signal(barrier, inc=1, device_id={"ctx": me, "head": 1 - core}, device_id_type=MESH)
+    cols[...] = jnp.transpose(flat[...])
+    doc_cols[G] = jnp.transpose(jnp.broadcast_to(doc_row, (DH, ROWS)))
     pl.semaphore_wait(barrier, 6)
 
     def v_copy(off):
@@ -152,21 +170,28 @@
     def up_copy(ref, ssem, rsem, b):
         return remote(ref.at[3 + b], ref.at[b - 1], ssem.at[b - 1], rsem.at[b - 1], up)
 
+    def own_v_up(b):
+        return remote(v_hbm.at[:, head_cols(b)], v_all.at[b - 1], vz_ssem.at[b - 1], v_rsem.at[b - 1], up)
+
+    def row_wait(b):
+        from_slot(v_all, v_ssem, v_rsem, 3 + b).wait_recv()
+        from_slot(doc_all, d_ssem, d_rsem, 3 + b).wait_recv()
+
+    def row_up(b):
+        up_copy(v_all, vz_ssem, v_rsem, b).start()
+        up_copy(doc_all, dz_ssem, d_rsem, b).start()
+
     w_copy = remote(w_hbm, w_got, w_sem.at[1], w_sem.at[2], None, 1 - core)
-    for off in (2, 1, 3):
+    for off in (1, 3, 2):
         v_copy(off).start()
+        doc_copy(off).start()
+    for b in (3, 2, 1):
+        @pl.when(x == b)
+        def _():
+            own_v_up(b).start()
+            up_copy(doc_all, dz_ssem, d_rsem, b).start()
     own_w.start()
     w_copy.start()
-
-    doc_row = doc_ref[...].astype(jnp.float32)
-    doc_own[...] = jnp.broadcast_to(doc_row, (8, ROWS))
-    flat[...] = jnp.zeros_like(flat)
-    flat[0:G, :] = beta_ref[...]
-    flat[8:16, :] = jnp.broadcast_to(doc_row, (8, ROWS))
-    cols[...] = jnp.transpose(flat[...])
-    doc_all[pl.ds(3 + x, 1)] = jnp.broadcast_to(doc_row, (8, ROWS))[None]
-    for off in (1, 2, 3):
-        doc_copy(off).start()
 
     lane = lax.broadcasted_iota(jnp.int32, (ROWS, DH), 1)
 
@@ -196,37 +221,31 @@
         @pl.when(it < G - 1)
         def _():
             ks_copy(off).start()
-            q_copy(off).start()
+
+        for step, phases in ((1, (1, 3)), (2, (2,))):
+            for b in (3, 2, 1):
+                @pl.when((it == step) & functools.reduce(lambda m, c: m | c, [lax.rem(x + G - b, G) == f for f in phases]))
+                def _():
+                    row_wait(b)
+                    row_up(b)
+
+    for off in (3, 2, 1):
+        q_copy(off).start()
 
     load(3, *loads[3], x).wait()
     v_all[pl.ds(3 + x, 1)] = v_in[pl.ds(x, 1)]
     ks_all[pl.ds(3 + x, 1)] = ks_send[pl.ds(x, 1)]
     q_all[pl.ds(x, 1)] = q_send[pl.ds(x, 1)]
 
-    for b in (3, 2, 1):
-        @pl.when(x != b)
-        def _():
-            from_slot(v_all, v_ssem, v_rsem, 3 + b).wait_recv()
-            from_slot(doc_all, d_ssem, d_rsem, 3 + b).wait_recv()
-        up_copy(v_all, vz_ssem, v_rsem, b).start()
-        up_copy(doc_all, dz_ssem, d_rsem, b).start()
-    for b in (3, 2, 1):
-        @pl.when(x != b)
-        def _():
-            from_slot(ks_all, ks_ssem, ks_rsem, 3 + b).wait_recv()
-        up_copy(ks_all, kz_ssem, ks_rsem, b).start()
-
     for off in (1, 2, 3):
         load(3, *loads[3], ring(off)).wait()
-    row, col = iotas(PIECE, PIECE)
-
-    @pl.loop(0, G)
-    def _(h):
+
+    def own_attention(h):
         for p in range(PIECES):
             here = slice(p * PIECE, (p + 1) * PIECE)
             width = (p + 1) * PIECE
             raw = scores[h, here, 0:width]
-            same = cols[here, 8:9] == doc_own[0:1, 0:width]
+            same = jnp.concatenate([doc_cols[G, here, :]] * (p + 1), axis=1) == doc_own[0:1, 0:width]
             wide_row, wide_col = iotas(PIECE, width)
             allowed = same & (wide_row + p * PIECE >= wide_col)
             masked = jnp.where(allowed, raw, MASKED)
@@ -236,12 +255,55 @@
             own_l[h, here] = jnp.sum(weights, axis=-1, keepdims=True)
             own_o[h, here] = dot(weights, v_in[h, 0:width])
 
-    b0 = (0,)
-    @pl.when(x != 0)
-    def _():
-        from_slot(v_all, v_ssem, v_rsem, 3).wait_recv()
-        from_slot(doc_all, d_ssem, d_rsem, 3).wait_recv()
-        from_slot(ks_all, ks_ssem, ks_rsem, 3).wait_recv()
+    @pl.loop(0, G)
+    def _(h):
+        own_attention(h)
+
+    def split_keys(slot):
+        high, low = split(ks_all[slot, 0:ROWS])
+        kb[slot] = jnp.concatenate([high, high, low], axis=1)
+
+    def split_values(slot):
+        high, low = split(v_all[slot])
+        vb[slot] = jnp.concatenate([high, low], axis=1)
+
+    def split_docs(b):
+        doc_cols[b] = jnp.transpose(jnp.broadcast_to(doc_all[3 + b, 0:1, :], (DH, ROWS)))
+
+    def ks_wait(b):
+        from_slot(ks_all, ks_ssem, ks_rsem, 3 + b).wait_recv()
+
+    for b in (3, 2, 1, 0):
+        @pl.when(x != b)
+        def _():
+            ks_wait(b)
+        if b > 0:
+            up_copy(ks_all, kz_ssem, ks_rsem, b).start()
+        else:
+            @pl.when(x != b)
+            def _():
+                row_wait(0)
+        if b < 3:
+            split_keys(3 + b)
+            split_values(3 + b)
+        split_docs(b)
+
+    depth = G * DH
+    own_w.wait()
+    w_copy.wait_recv()
+
+    @pl.loop(0, 2 * depth // PIECE)
+    def _(i):
+        at = pl.ds(pl.multiple_of(lax.rem(i, G) * PIECE, PIECE), PIECE)
+        to = pl.ds(pl.multiple_of(i * PIECE, PIECE), PIECE)
+
+        @pl.when(i < G)
+        def _():
+            w_high[to, :], w_low[to, :] = split(w_own[at, :])
+
+        @pl.when(i >= G)
+        def _():
+            w_high[to, :], w_low[to, :] = split(w_got[at, :])
 
     def o_copy(b, slot):
         return remote(cross_o.at[b], ret_o.at[slot], o_ssem.at[b], o_rsem.at[slot], row_start + b)
@@ -260,32 +322,40 @@
             halo = b
             up_copy(v_all, vz_ssem, v_rsem, halo + 1).wait_recv()
             up_copy(doc_all, dz_ssem, d_rsem, halo + 1).wait_recv()
+            split_values(halo)
             up_copy(ks_all, kz_ssem, ks_rsem, halo + 1).wait_recv()
-        flat[0:8, :] = doc_all[slot]
-        doc_col = jnp.transpose(flat[...])[:, 0:1]
+            split_keys(halo)
         key_docs = []
+        current = q_all[b]
         for d in (1, 2, 3):
             key_doc = doc_all[slot - d, 0:1, :]
             if slot - d < 3:
                 key_doc = jnp.where(me >= G, key_doc, -1.0)
             key_docs.append(key_doc)
-        current = q_all[b]
-        raws = []
-        for d in (1, 2, 3):
             if d > 1:
                 current = dot(current, ks_all[slot - d + 1, ROWS : ROWS + DH], 1, 1)
-            raw = dot(current, ks_all[slot - d, 0:ROWS], 1, 1)
-            raws.append(jnp.where(doc_col == key_docs[d - 1], raw, MASKED))
-        peak = functools.reduce(jnp.maximum, [jnp.max(r, axis=-1, keepdims=True) for r in raws])
-        total = jnp.zeros((ROWS, 1), jnp.float32)
-        summed = jnp.zeros((ROWS, DH), jnp.float32)
-        for d in (1, 2, 3):
-            weights = jnp.exp2(raws[d - 1] - peak)
-            total = total + jnp.sum(weights, axis=-1, keepdims=True)
-            summed = summed + dot(weights, v_all[slot - d])
-        cross_o[b] = summed
-        stats = jnp.where(lane == 0, peak, jnp.where(lane == 1, total, 0.0))
-        cross_st[b] = jnp.transpose(stats)[0:8, :]
+            high, low = split(current)
+            qb[d - 1] = jnp.concatenate([high, low, high], axis=1)
+        chunk = ROWS // 2
+        for start in (0, chunk):
+            here = slice(start, start + chunk)
+            doc_col = jnp.concatenate([doc_cols[b, here, :]] * (ROWS // DH), axis=1)
+            raws = [
+                jnp.where(doc_col == key_docs[d - 1], half_dot(qb[d - 1, here], kb[slot - d], 1, 1), MASKED)
+                for d in (1, 2, 3)
+            ]
+            peak = functools.reduce(jnp.maximum, [jnp.max(r, axis=-1, keepdims=True) for r in raws])
+            total = jnp.zeros((chunk, 1), jnp.float32)
+            summed = jnp.zeros((chunk, DH), jnp.float32)
+            for d in (1, 2, 3):
+                weights = jnp.exp2(raws[d - 1] - peak)
+                total = total + jnp.sum(weights, axis=-1, keepdims=True)
+                high, low = split(weights)
+                both = half_dot(high, vb[slot - d])
+                summed = summed + both[:, :DH] + both[:, DH:] + half_dot(low, vb[slot - d, :, 0:DH])
+            cross_o[b, here] = summed
+            stats = jnp.where(lane[:chunk] == 0, peak, jnp.where(lane[:chunk] == 1, total, 0.0))
+            cross_st[b, :, here] = jnp.transpose(stats)[0:8, :]
 
         @pl.when(x != b)
         def _():
@@ -317,17 +387,20 @@
     other_rows = pl.ds(pl.multiple_of((1 - core) * half, half), half)
     a_copy = remote(att.at[other_rows], att_got, a_sem.at[0], a_sem.at[1], None, 1 - core)
     a_copy.start()
-    own_w.wait()
     tile = 512
-    for j in range(4):
-        at = slice(j * tile, (j + 1) * tile)
-        out_ref[:, at] = dot(att[mine_rows, :], w_own[:, at])
-    w_copy.wait()
-    a_copy.wait()
-    for j in range(4):
-        at = slice(j * tile, (j + 1) * tile)
-        out_ref[:, at] = out_ref[:, at] + dot(att_got[...], w_got[:, at])
-
+    for part in range(2):
+        if part == 1:
+            a_copy.wait()
+        high, low = split(att[mine_rows, :] if part == 0 else att_got[...])
+        both = jnp.concatenate([high, low], axis=1)
+        rows = slice(part * depth, (part + 1) * depth)
+        for j in range(4):
+            at = slice(j * tile, (j + 1) * tile)
+            weight = w_high[rows, at]
+            term = half_dot(both, jnp.concatenate([weight, weight], axis=0)) + half_dot(high, w_low[rows, at])
+            out_ref[:, at] = term if part == 0 else out_ref[:, at] + term
+
+    w_copy.wait_send()
     for off in (1, 2, 3):
         v_copy(off).wait_send()
         doc_copy(off).wait_send()
@@ -359,12 +432,16 @@
         scratch_shapes=[
             heads, heads, heads, heads,
             pltpu.VMEM((DH, ROWS), f32), pltpu.VMEM((ROWS, DH), f32), pltpu.VMEM((8, ROWS), f32),
+            pltpu.VMEM((G + 1, ROWS, DH), f32),
             pltpu.VMEM((G, ROWS, ROWS), f32), pltpu.VMEM((G, ROWS + DH, DH), f32), heads,
             pltpu.VMEM((7, ROWS, DH), f32), pltpu.VMEM((7, ROWS + DH, DH), f32), heads, pltpu.VMEM((7, 8, ROWS), f32),
             heads, pltpu.VMEM((G, ROWS, 1), f32), pltpu.VMEM((G, ROWS, 1), f32),
             heads, pltpu.VMEM((G, 8, ROWS), f32), heads, pltpu.VMEM((G, 8, ROWS), f32),
             pltpu.VMEM((ROWS, G * DH), f32), pltpu.VMEM((ROWS // 2, G * DH), f32),
             pltpu.VMEM((G * DH, columns), f32), pltpu.VMEM((G * DH, columns), f32),
+            pltpu.VMEM((2 * G * DH, columns), jnp.bfloat16), pltpu.VMEM((2 * G * DH, columns), jnp.bfloat16),
+            pltpu.VMEM((7, ROWS, 3 * DH), jnp.bfloat16), pltpu.VMEM((7, ROWS, 2 * DH), jnp.bfloat16),
+            pltpu.VMEM((3, ROWS, 3 * DH), jnp.bfloat16),
             dma((4, G)), dma((4,)), dma((7,)), dma((4,)), dma((7,)), dma((4,)), dma((4,)), dma((4,)), dma((7,)),
             dma((3,)), dma((3,)), dma((3,)), dma((4,)), dma((4,)), dma((4,)), dma((4,)), dma((3,)), dma((2,)),
         ],

time: 99.6 us -> 78.8 us (0.79)
  Pallas kernels: 96.2 us -> 75.5 us
    pallas_call x1, Pallas kernels: 96.2 us -> 75.5 us  [shards(): pl.pallas_call(functools.partial(kernel, n), out_shape=jax.ShapeDtypeStru...]
where the time goes in v2:
time: 78.8 us; the launch traced here: 78.7 us
  Pallas kernels  75.5 us (96%)
  local copies, waits for them, and re-layouts  3.14 us (4%)
    pallas_call x1, Pallas kernels, shards(): pl.pallas_call(functools.partial(kernel, n), out_shape=jax.ShapeDtypeStru...  75.5 us
    unnamed x1, local copies, waits for them, and re-layouts  3.14 us

profile of v2, /device:TPU:1, one launch (start us, length us, event | category | flops | bytes accessed | tf_op | source)
XLA Modules:
  0.0 78.7 jit_solution(6809890104683520924)
XLA Ops:
  0.0 75.5 %path_layer.1 = f32[256,2048]{1,0:T(8,128)} custom-call(f32[512,512]{1,0:T(8,128)} %q_hbm.1, f32[512,512]{1,0:T(8,128)} %k_hbm.1, f32[512,512]{1,0:T(8,128)} %v_hbm.1, f32[512,512]{1,0:T(8,128)} %t_hbm.1, f32[4,512]{1,0:T(4,128)} %beta_ref.1, s32[1,512]{1,0:T(1,128)} %bitcast.1, f32[512,2048]{1,0:T(8,128)} %w_hbm.1), custom_call_target="tpu_custom_call" | custom-call | tf_op jit(solution)/shard_map/path_layer/pallas_call | solution.py:427
  75.5 3.1 %copy.9 = f32[256,2048]{1,0:T(8,128)} copy(f32[256,2048]{1,0:T(8,128)} %path_layer.1) | data formatting | bytes 4194304

commit v3 on v2

--- a/solution.py
+++ b/solution.py
@@ -16,6 +16,8 @@
 PIECE = 128
 PIECES = ROWS // PIECE
 MASKED = -1e30
+ORDER = ((3, 3, 3, 3), (2, 2, 2, 2), (1, 1, 1, 1), (0, 0, 0, 0))
+HALOS = ((), (2,), (1,), (0,))
 
 
 def dot(left, right, left_dim=1, right_dim=0):
@@ -97,11 +99,11 @@
     q_in, k_in, t_in, v_in, flat, cols, doc_own, doc_cols,
     scores, ks_send, q_send,
     v_all, ks_all, q_all, doc_all,
-    own_o, own_m, own_l,
+    own_o, own_st,
     cross_o, cross_st, ret_o, ret_st,
     att, att_got, w_own, w_got, w_high, w_low, kb, vb, qb,
     in_sem, v_ssem, v_rsem, ks_ssem, ks_rsem, q_ssem, q_rsem, d_ssem, d_rsem,
-    vz_ssem, kz_ssem, dz_ssem, o_ssem, o_rsem, s_ssem, s_rsem, w_sem, a_sem,
+    vz_ssem, kz_ssem, dz_ssem, o_ssem, o_rsem, s_ssem, s_rsem, w_sem, a_ssem, a_rsem,
 ):
     me = lax.axis_index("ctx")
     core = lax.axis_index("head")
@@ -167,6 +169,10 @@
     def from_slot(ref, ssem, rsem, slot):
         return remote(ref.at[slot], ref.at[slot], ssem.at[0], rsem.at[slot], row_start)
 
+    def ks_up(b):
+        rows = slice(0, ROWS if b == 1 else ROWS + DH)
+        return remote(ks_all.at[3 + b, rows], ks_all.at[b - 1, rows], kz_ssem.at[b - 1], ks_rsem.at[b - 1], up)
+
     def up_copy(ref, ssem, rsem, b):
         return remote(ref.at[3 + b], ref.at[b - 1], ssem.at[b - 1], rsem.at[b - 1], up)
 
@@ -182,8 +188,9 @@
         up_copy(doc_all, dz_ssem, d_rsem, b).start()
 
     w_copy = remote(w_hbm, w_got, w_sem.at[1], w_sem.at[2], None, 1 - core)
+    for off in (1, 3):
+        v_copy(off).start()
     for off in (1, 3, 2):
-        v_copy(off).start()
         doc_copy(off).start()
     for b in (3, 2, 1):
         @pl.when(x == b)
@@ -222,6 +229,10 @@
         def _():
             ks_copy(off).start()
 
+        @pl.when(it == 0)
+        def _():
+            v_copy(2).start()
+
         for step, phases in ((1, (1, 3)), (2, (2,))):
             for b in (3, 2, 1):
                 @pl.when((it == step) & functools.reduce(lambda m, c: m | c, [lax.rem(x + G - b, G) == f for f in phases]))
@@ -251,8 +262,9 @@
             masked = jnp.where(allowed, raw, MASKED)
             peak = jnp.max(masked, axis=-1, keepdims=True)
             weights = jnp.exp2(masked - peak)
-            own_m[h, here] = peak
-            own_l[h, here] = jnp.sum(weights, axis=-1, keepdims=True)
+            total = jnp.sum(weights, axis=-1, keepdims=True)
+            stats = jnp.where(lane[:PIECE] == 0, peak, jnp.where(lane[:PIECE] == 1, total, 0.0))
+            own_st[h, :, here] = jnp.transpose(stats)[0:8, :]
             own_o[h, here] = dot(weights, v_in[h, 0:width])
 
     @pl.loop(0, G)
@@ -278,7 +290,7 @@
         def _():
             ks_wait(b)
         if b > 0:
-            up_copy(ks_all, kz_ssem, ks_rsem, b).start()
+            ks_up(b).start()
         else:
             @pl.when(x != b)
             def _():
@@ -305,35 +317,39 @@
         def _():
             w_high[to, :], w_low[to, :] = split(w_got[at, :])
 
-    def o_copy(b, slot):
-        return remote(cross_o.at[b], ret_o.at[slot], o_ssem.at[b], o_rsem.at[slot], row_start + b)
-
-    def st_copy(b, slot):
-        return remote(cross_st.at[b], ret_st.at[slot], s_ssem.at[b], s_rsem.at[slot], row_start + b)
-
-    for b in (3, 2, 1, 0):
-        slot = 3 + b
+    def o_copy(b, part):
+        rows = slice(part * half, (part + 1) * half)
+        return remote(
+            cross_o.at[b, rows], ret_o.at[x, rows], o_ssem.at[b, part], o_rsem.at[x, part], row_start + b
+        )
+
+    def st_copy(b):
+        return remote(cross_st.at[b], ret_st.at[x], s_ssem.at[b], s_rsem.at[x], row_start + b)
+
+    for turn, order in enumerate(ORDER):
+        table = sum(b << (2 * i) for i, b in enumerate(order))
+        b = (table >> (2 * x)) & 3
+        place = 3 + b
 
         @pl.when(x != b)
         def _():
             from_slot(q_all, q_ssem, q_rsem, b).wait_recv()
 
-        if b < 3:
-            halo = b
+        for halo in HALOS[turn]:
             up_copy(v_all, vz_ssem, v_rsem, halo + 1).wait_recv()
             up_copy(doc_all, dz_ssem, d_rsem, halo + 1).wait_recv()
+            ks_up(halo + 1).wait_recv()
             split_values(halo)
-            up_copy(ks_all, kz_ssem, ks_rsem, halo + 1).wait_recv()
             split_keys(halo)
+
         key_docs = []
         current = q_all[b]
         for d in (1, 2, 3):
-            key_doc = doc_all[slot - d, 0:1, :]
-            if slot - d < 3:
-                key_doc = jnp.where(me >= G, key_doc, -1.0)
-            key_docs.append(key_doc)
+            slot = place - d
+            exists = (slot >= 3) | (me >= G)
+            key_docs.append(jnp.where(exists, doc_all[slot, 0:1, :], -1.0))
             if d > 1:
-                current = dot(current, ks_all[slot - d + 1, ROWS : ROWS + DH], 1, 1)
+                current = dot(current, ks_all[slot + 1, ROWS : ROWS + DH], 1, 1)
             high, low = split(current)
             qb[d - 1] = jnp.concatenate([high, low, high], axis=1)
         chunk = ROWS // 2
@@ -341,7 +357,7 @@
             here = slice(start, start + chunk)
             doc_col = jnp.concatenate([doc_cols[b, here, :]] * (ROWS // DH), axis=1)
             raws = [
-                jnp.where(doc_col == key_docs[d - 1], half_dot(qb[d - 1, here], kb[slot - d], 1, 1), MASKED)
+                jnp.where(doc_col == key_docs[d - 1], half_dot(qb[d - 1, here], kb[place - d], 1, 1), MASKED)
                 for d in (1, 2, 3)
             ]
             peak = functools.reduce(jnp.maximum, [jnp.max(r, axis=-1, keepdims=True) for r in raws])
@@ -351,54 +367,77 @@
                 weights = jnp.exp2(raws[d - 1] - peak)
                 total = total + jnp.sum(weights, axis=-1, keepdims=True)
                 high, low = split(weights)
-                both = half_dot(high, vb[slot - d])
-                summed = summed + both[:, :DH] + both[:, DH:] + half_dot(low, vb[slot - d, :, 0:DH])
+                both = half_dot(high, vb[place - d])
+                summed = summed + both[:, :DH] + both[:, DH:] + half_dot(low, vb[place - d, :, 0:DH])
             cross_o[b, here] = summed
+
+            @pl.when(x != b)
+            def _():
+                o_copy(b, start // chunk).start()
+
             stats = jnp.where(lane[:chunk] == 0, peak, jnp.where(lane[:chunk] == 1, total, 0.0))
             cross_st[b, :, here] = jnp.transpose(stats)[0:8, :]
 
         @pl.when(x != b)
         def _():
-            o_copy(b, x).start()
-            st_copy(b, x).start()
+            st_copy(b).start()
 
         @pl.when(x == b)
         def _():
-            ret_o[pl.ds(x, 1)] = cross_o[b][None]
-            ret_st[pl.ds(x, 1)] = cross_st[b][None]
-
-    for off in (1, 2, 3):
-        h = ring(off)
-        remote(ret_o.at[h], ret_o.at[h], o_ssem.at[0], o_rsem.at[h], row_start).wait_recv()
-        remote(ret_st.at[h], ret_st.at[h], s_ssem.at[0], s_rsem.at[h], row_start).wait_recv()
-    for h in range(G):
-        flat[8 * h : 8 * h + 8, :] = ret_st[h]
-    stat_cols = jnp.transpose(flat[...])
-    for h in range(G):
-        other_m = stat_cols[:, 8 * h : 8 * h + 1]
-        other_l = stat_cols[:, 8 * h + 1 : 8 * h + 2]
-        peak = jnp.maximum(own_m[h], other_m)
-        mine = jnp.exp2(own_m[h] - peak)
-        other = jnp.exp2(other_m - peak)
-        total = mine * own_l[h] + other * other_l
-        att[:, h * DH : (h + 1) * DH] = (mine * own_o[h] + other * ret_o[h]) / total
+            ret_o[pl.ds(x, 1)] = cross_o[pl.ds(b, 1)]
+            ret_st[pl.ds(x, 1)] = cross_st[pl.ds(b, 1)]
 
     mine_rows = pl.ds(pl.multiple_of(core * half, half), half)
     other_rows = pl.ds(pl.multiple_of((1 - core) * half, half), half)
-    a_copy = remote(att.at[other_rows], att_got, a_sem.at[0], a_sem.at[1], None, 1 - core)
-    a_copy.start()
-    tile = 512
-    for part in range(2):
-        if part == 1:
-            a_copy.wait()
-        high, low = split(att[mine_rows, :] if part == 0 else att_got[...])
-        both = jnp.concatenate([high, low], axis=1)
-        rows = slice(part * depth, (part + 1) * depth)
+
+    def a_copy(h):
+        return remote(att.at[h, other_rows], att_got.at[h], a_ssem.at[h], a_rsem.at[h], None, 1 - core)
+
+    def wide(row_values):
+        return jnp.transpose(jnp.broadcast_to(row_values, (DH, ROWS)))
+
+    def join(h):
+        own_m, own_l = own_st[h, 0:1, :], own_st[h, 1:2, :]
+        other_m, other_l = ret_st[h, 0:1, :], ret_st[h, 1:2, :]
+        peak = jnp.maximum(own_m, other_m)
+        mine = jnp.exp2(own_m - peak)
+        other = jnp.exp2(other_m - peak)
+        total = mine * own_l + other * other_l
+        att[h] = wide(mine / total) * own_o[h] + wide(other / total) * ret_o[h]
+        a_copy(h).start()
+
+    def project(parts, add):
+        pairs = [split(rows) for rows, _ in parts]
+        lefts = [jnp.concatenate([high, low], axis=1) for high, low in pairs]
+        both = jnp.concatenate(lefts, axis=1)
+        highs = jnp.concatenate([high for high, _ in pairs], axis=1)
+        tile = 512
         for j in range(4):
             at = slice(j * tile, (j + 1) * tile)
-            weight = w_high[rows, at]
-            term = half_dot(both, jnp.concatenate([weight, weight], axis=0)) + half_dot(high, w_low[rows, at])
-            out_ref[:, at] = term if part == 0 else out_ref[:, at] + term
+            weights = [w_high[pl.ds(begin, DH), at] for _, begin in parts]
+            lows = [w_low[pl.ds(begin, DH), at] for _, begin in parts]
+            doubled = jnp.concatenate([w for weight in weights for w in (weight, weight)], axis=0)
+            term = half_dot(both, doubled) + half_dot(highs, jnp.concatenate(lows, axis=0))
+            out_ref[:, at] = out_ref[:, at] + term if add else term
+
+    def begin(h, mine):
+        return pl.multiple_of(h * DH + (0 if mine else depth), DH)
+
+    for group in ((0, 1, 3, 2),):
+        heads = [ring(off) for off in group]
+        for h, off in zip(heads, group):
+            if off > 0:
+                for part in range(2):
+                    rows = slice(part * half, (part + 1) * half)
+                    remote(
+                        ret_o.at[h, rows], ret_o.at[h, rows], o_ssem.at[0, part], o_rsem.at[h, part], row_start
+                    ).wait_recv()
+                remote(ret_st.at[h], ret_st.at[h], s_ssem.at[0], s_rsem.at[h], row_start).wait_recv()
+            join(h)
+        project([(att[h, mine_rows, :], begin(h, True)) for h in heads], False)
+        for h in heads:
+            a_copy(h).wait_recv()
+        project([(att_got[h], begin(h, False)) for h in heads], True)
 
     w_copy.wait_send()
     for off in (1, 2, 3):
@@ -409,12 +448,16 @@
     for b in (1, 2, 3):
         up_copy(v_all, vz_ssem, v_rsem, b).wait_send()
         up_copy(doc_all, dz_ssem, d_rsem, b).wait_send()
-        up_copy(ks_all, kz_ssem, ks_rsem, b).wait_send()
+        ks_up(b).wait_send()
     for b in range(G):
         @pl.when(x != b)
         def _():
-            o_copy(b, x).wait_send()
-            st_copy(b, x).wait_send()
+            o_copy(b, 0).wait_send()
+            o_copy(b, 1).wait_send()
+            st_copy(b).wait_send()
+
+    for h in range(G):
+        a_copy(h).wait_send()
 
 
 def shards(n, queries, keys, values, transitions, betas, documents, out_weight):
@@ -435,15 +478,15 @@
             pltpu.VMEM((G + 1, ROWS, DH), f32),
             pltpu.VMEM((G, ROWS, ROWS), f32), pltpu.VMEM((G, ROWS + DH, DH), f32), heads,
             pltpu.VMEM((7, ROWS, DH), f32), pltpu.VMEM((7, ROWS + DH, DH), f32), heads, pltpu.VMEM((7, 8, ROWS), f32),
-            heads, pltpu.VMEM((G, ROWS, 1), f32), pltpu.VMEM((G, ROWS, 1), f32),
+            heads, pltpu.VMEM((G, 8, ROWS), f32),
             heads, pltpu.VMEM((G, 8, ROWS), f32), heads, pltpu.VMEM((G, 8, ROWS), f32),
-            pltpu.VMEM((ROWS, G * DH), f32), pltpu.VMEM((ROWS // 2, G * DH), f32),
+            heads, pltpu.VMEM((G, ROWS // 2, DH), f32),
             pltpu.VMEM((G * DH, columns), f32), pltpu.VMEM((G * DH, columns), f32),
             pltpu.VMEM((2 * G * DH, columns), jnp.bfloat16), pltpu.VMEM((2 * G * DH, columns), jnp.bfloat16),
             pltpu.VMEM((7, ROWS, 3 * DH), jnp.bfloat16), pltpu.VMEM((7, ROWS, 2 * DH), jnp.bfloat16),
             pltpu.VMEM((3, ROWS, 3 * DH), jnp.bfloat16),
             dma((4, G)), dma((4,)), dma((7,)), dma((4,)), dma((7,)), dma((4,)), dma((4,)), dma((4,)), dma((7,)),
-            dma((3,)), dma((3,)), dma((3,)), dma((4,)), dma((4,)), dma((4,)), dma((4,)), dma((3,)), dma((2,)),
+            dma((3,)), dma((3,)), dma((3,)), dma((4, 2)), dma((4, 2)), dma((4,)), dma((4,)), dma((3,)), dma((4,)), dma((4,)),
         ],
         compiler_params=pltpu.CompilerParams(
             collective_id=0, has_side_effects=True, vmem_limit_bytes=60 * 2**20

time: 78.8 us -> 76.3 us (0.968)
  Pallas kernels: 75.5 us -> 73 us
    pallas_call x1, Pallas kernels: 75.5 us -> 73 us  [shards(): pl.pallas_call(functools.partial(kernel, n), out_shape=jax.ShapeDtypeStru...]
where the time goes in v3:
time: 76.3 us; the launch traced here: 76.2 us
  Pallas kernels  73 us (96%)
  local copies, waits for them, and re-layouts  3.14 us (4%)
    pallas_call x1, Pallas kernels, shards(): pl.pallas_call(functools.partial(kernel, n), out_shape=jax.ShapeDtypeStru...  73 us
    unnamed x1, local copies, waits for them, and re-layouts  3.14 us

profile of v3, /device:TPU:1, one launch (start us, length us, event | category | flops | bytes accessed | tf_op | source)
XLA Modules:
  0.0 76.2 jit_solution(1618409096683291505)
XLA Ops:
  0.0 73.0 %path_layer.1 = f32[256,2048]{1,0:T(8,128)} custom-call(f32[512,512]{1,0:T(8,128)} %q_hbm.1, f32[512,512]{1,0:T(8,128)} %k_hbm.1, f32[512,512]{1,0:T(8,128)} %v_hbm.1, f32[512,512]{1,0:T(8,128)} %t_hbm.1, f32[4,512]{1,0:T(4,128)} %beta_ref.1, s32[1,512]{1,0:T(1,128)} %bitcast.1, f32[512,2048]{1,0:T(8,128)} %w_hbm.1), custom_call_target="tpu_custom_call" | custom-call | tf_op jit(solution)/shard_map/path_layer/pallas_call | solution.py:470
  73.0 3.1 %copy.9 = f32[256,2048]{1,0:T(8,128)} copy(f32[256,2048]{1,0:T(8,128)} %path_layer.1) | data formatting | bytes 4194304

commit v4 on v3

--- a/solution.py
+++ b/solution.py
@@ -285,7 +285,7 @@
     def ks_wait(b):
         from_slot(ks_all, ks_ssem, ks_rsem, 3 + b).wait_recv()
 
-    for b in (3, 2, 1, 0):
+    for b in (2, 3, 1, 0):
         @pl.when(x != b)
         def _():
             ks_wait(b)

time: 76.3 us -> 78.6 us (1.030)
  Pallas kernels: 73 us -> 75.3 us
    pallas_call x1, Pallas kernels: 73 us -> 75.3 us  [shards(): pl.pallas_call(functools.partial(kernel, n), out_shape=jax.ShapeDtypeStru...]
where the time goes in v4:
time: 78.6 us; the launch traced here: 78.5 us
  Pallas kernels  75.3 us (96%)
  local copies, waits for them, and re-layouts  3.14 us (4%)
    pallas_call x1, Pallas kernels, shards(): pl.pallas_call(functools.partial(kernel, n), out_shape=jax.ShapeDtypeStru...  75.3 us
    unnamed x1, local copies, waits for them, and re-layouts  3.14 us

profile of v4, /device:TPU:1, one launch (start us, length us, event | category | flops | bytes accessed | tf_op | source)
XLA Modules:
  0.0 78.5 jit_solution(7220207902144214599)
XLA Ops:
  0.0 75.3 %path_layer.1 = f32[256,2048]{1,0:T(8,128)} custom-call(f32[512,512]{1,0:T(8,128)} %q_hbm.1, f32[512,512]{1,0:T(8,128)} %k_hbm.1, f32[512,512]{1,0:T(8,128)} %v_hbm.1, f32[512,512]{1,0:T(8,128)} %t_hbm.1, f32[4,512]{1,0:T(4,128)} %beta_ref.1, s32[1,512]{1,0:T(1,128)} %bitcast.1, f32[512,2048]{1,0:T(8,128)} %w_hbm.1), custom_call_target="tpu_custom_call" | custom-call | tf_op jit(solution)/shard_map/path_layer/pallas_call | solution.py:470
  75.3 3.1 %copy.9 = f32[256,2048]{1,0:T(8,128)} copy(f32[256,2048]{1,0:T(8,128)} %path_layer.1) | data formatting | bytes 4194304
